TPU v7x, 512 devices: a whole 4x8x8 slice. The times are simulated.
512 devices in a mesh: src: 16 (over y, core), tgt: 32 (over x, z).
Axes of the slice: x: 4, y: 8, z: 8, core: 2. Of those that a mesh axis runs over, the one named last changes fastest.
Arguments:
- noise: float32 [16384, 384], P(('src', 'tgt')), may hold values from -16 to 16
- data: float32 [32768, 384], P('tgt', 'src'), may hold values from -6 to 6
Outputs:
- velocity: float32 [16384, 384], P(('src', 'tgt'))
- target_potential: float32 [32768], P('tgt')
All inputs are finite; a program needn't handle non-finite values.
Results may differ from a plain program's by a relative error of at most 0.0003.
Values sent between devices are 32-bit elements; how exact they have to be, the bound alone decides.
No kernel may reach another device: no remote copies, remote signals or barrier semaphores. Data moves between devices by JAX's collectives and lax.ppermute only.
A program may use at most 64 MiB of HBM per device.

v0:
```python
import math
import jax
import jax.numpy as jnp
from jax import lax
from jax.sharding import PartitionSpec as P

ITERS = 3
EPS = 0.05


def spread(value, axis):
    count = lax.axis_size(axis)
    return lax.all_to_all(jnp.broadcast_to(value[None], (count,) + value.shape), axis, 0, 0)


def total_over(local_sum, axis):
    tiles = local_sum.reshape(-1, 128)
    return jnp.sum(spread(tiles, axis), axis=0).reshape(local_sum.shape)


def lse_over(local_top, local_sum, axis):
    tiles = spread((local_top + jnp.log(local_sum)).reshape(-1, 128), axis)
    top = jnp.max(tiles, axis=0)
    merged = top + jnp.log(jnp.sum(jnp.exp(tiles - top[None]), axis=0))
    return merged.reshape(local_top.shape)


def per_device(noise, data):
    target_rows = lax.all_gather(data, "src", axis=1, tiled=True)
    own_rows, feat_width = noise.shape
    source_rows = spread(noise, "tgt").reshape(-1, feat_width)
    src_total = source_rows.shape[0] * lax.axis_size("src")
    tgt_total = target_rows.shape[0] * lax.axis_size("tgt")
    source_sq = jnp.sum(source_rows * source_rows, axis=1)
    target_sq = jnp.sum(target_rows * target_rows, axis=1)
    cross = jnp.dot(
        source_rows,
        target_rows.T,
        precision=lax.Precision.HIGHEST,
        preferred_element_type=jnp.float32,
    )
    gain = (2.0 * cross - source_sq[:, None] - target_sq[None, :]) / (feat_width * EPS)
    log_src, log_tgt = (math.log(src_total), math.log(tgt_total))
    top = jnp.max(gain, axis=1)
    f_pot = -(log_src + lse_over(top, jnp.sum(jnp.exp(gain - top[:, None]), axis=1), "tgt"))
    z_tile = f_pot[:, None] + gain
    top = jnp.max(z_tile, axis=0)
    g_pot = -(log_tgt + lse_over(top, jnp.sum(jnp.exp(z_tile - top[None, :]), axis=0), "src"))
    for step_index in range(1, ITERS):
        mass = jnp.sum(jnp.exp(f_pot[:, None] + gain + g_pot[None, :]), axis=1)
        f_pot = f_pot - (log_src + jnp.log(total_over(mass, "tgt")))
        mass = jnp.sum(jnp.exp(f_pot[:, None] + gain + g_pot[None, :]), axis=0)
        g_pot = g_pot - (log_tgt + jnp.log(total_over(mass, "src")))
    plan = jnp.exp(f_pot[:, None] + gain + g_pot[None, :])
    mass = jnp.sum(plan, axis=1)
    part = jnp.dot(
        plan, target_rows, precision=lax.Precision.HIGHEST, preferred_element_type=jnp.float32
    )
    count = lax.axis_size("tgt")
    part = lax.all_to_all(part.reshape(count, own_rows, feat_width), "tgt", 0, 0)
    mass = lax.all_to_all(mass.reshape(count, own_rows), "tgt", 0, 0)
    bary = jnp.sum(part, axis=0) / jnp.sum(mass, axis=0)[:, None]
    return (bary - noise, EPS * g_pot)


def solution(mesh):
    placed = (P(("src", "tgt"), None), P("tgt", "src"))
    return jax.shard_map(
        per_device,
        mesh=mesh,
        in_specs=placed,
        out_specs=(P(("src", "tgt"), None), P("tgt")),
        check_vma=False,
    )
```

profile of v0, /device:TPU:8, one launch (start us, length us, event | category | flops | bytes accessed | tf_op | source)
XLA Modules:
  0.0 251.7 jit_solution(776631761340296787)
XLA Ops:
  7.2 0.0 all-gather.2.cloned.1.call-start
  7.2 0.7 all-gather.2.cloned.1.call-update
  7.9 2.1 broadcast_in_dim.22
  10.0 13.2 %all-to-all-start = ((f32[32,32,384]{2,1,0:T(8,128)}), f32[32,32,384]{2,1,0:T(8,128)S(1)}, u32[]{:S(2)}, u32[]{:S(2)}) async-start(f32[32,32,384]{2,1,0:T(8,128)} %broadcast_in_dim.22), calls=%async_computation | async-start | bytes 3145728 | tf_op jit(solution)/shard_map/all_to_all | solution.py:13
  23.2 32.4 %all-gather.2.cloned.1.call-done = f32[1024,384]{0,1:T(8,128)} async-done(((f32[1024,24]{0,1:T(8,128)}), f32[1024,384]{0,1:T(8,128)}) %all-gather.2.cloned.1.call-update) | async-done | bytes 1572880 | tf_op jit(solution)/shard_map/all_gather | solution.py:29
  55.6 1.5 multiply_reduce_fusion
  57.1 5.4 %all-to-all-done = f32[32,32,384]{2,1,0:T(8,128)S(1)} async-done(((f32[32,32,384]{2,1,0:T(8,128)}), f32[32,32,384]{2,1,0:T(8,128)S(1)}, u32[]{:S(2)}, u32[]{:S(2)}) %all-to-all-start) | async-done | bytes 1572896 | tf_op jit(solution)/shard_map/all_to_all | solution.py:13
  62.5 0.2 multiply_reduce_fusion.1
  62.8 0.1 sub.87
  62.8 8.9 %fusion.4 = (f32[1024]{0:T(1024)S(1)}, f32[1024,1024]{0,1:T(8,128)S(1)}) fusion(f32[1024]{0:T(1024)S(1)} %multiply_reduce_fusion, f32[1024]{0:T(1024)S(1)} %sub.87, f32[1024,384]{1,0:T(8,128)S(1)} %bitcast.27, f32[1024,384]{0,1:T(8,128)} %all-gather.2.cloned.1.call-done), kind=kOutput, calls=%fused_computation.27 | convolution fusion | flops 4837080064 | bytes 7352320 | tf_op jit(solution)/shard_map/dot_general | solution.py:36
  71.7 0.0 copy-start
  71.7 1.9 copy-done
  73.6 0.6 exponential_reduce_fusion.5
  74.3 15.8 %all_to_all.49 = f32[32,8,128]{2,1,0:T(8,128)S(1)} all-to-all(f32[32,8,128]{2,1,0:T(8,128)S(1)} %broadcast_in_dim.23), channel_id=1, replica_groups=mesh['src'=16,'tgt'=32] {'tgt'}, dimensions={0} | all-to-all | bytes 262144 | tf_op jit(solution)/shard_map/all_to_all | solution.py:13
  90.1 0.0 copy-start.1
  90.2 2.7 %add_reduce_fusion = f32[1024]{0:T(1024)S(1)} fusion(f32[1024,1024]{0,1:T(8,128)} %copy-done, f32[1024]{0:T(1024)S(1)} %negate_bitcast_fusion.1), kind=kLoop, calls=%fused_computation.8 | loop fusion | flops 2096128 | bytes 4202496 | tf_op jit(solution)/shard_map/reduce_max | solution.py:47
  92.8 0.7 copy-done.1
  93.5 0.9 exponential_reduce_fusion.4
  94.5 13.9 %all_to_all.50 = f32[16,8,128]{2,1,0:T(8,128)S(1)} all-to-all(f32[16,8,128]{2,1,0:T(8,128)S(1)} %broadcast_in_dim.24), channel_id=1, replica_groups=mesh['src'=16,'tgt'=32] {'src'}, dimensions={0} | all-to-all | bytes 131072 | tf_op jit(solution)/shard_map/all_to_all | solution.py:13
  108.5 2.9 %exponential_reduce_fusion.3 = f32[1024]{0:T(1024)S(1)} fusion(f32[1024,1024]{0,1:T(8,128)} %copy-done, f32[1024]{0:T(1024)S(1)} %negate_bitcast_fusion, f32[1024]{0:T(1024)S(1)} %negate_bitcast_fusion.1), kind=kLoop, calls=%fused_computation.4 | loop fusion | flops 3144704 | bytes 4206592 | tf_op jit(solution)/shard_map/reduce_sum | solution.py:50
  111.4 14.2 %all_to_all.51 = f32[32,8,128]{2,1,0:T(8,128)S(1)} all-to-all(f32[32,8,128]{2,1,0:T(8,128)S(1)} %broadcast_in_dim.26), channel_id=1, replica_groups=mesh['src'=16,'tgt'=32] {'tgt'}, dimensions={0} | all-to-all | bytes 262144 | tf_op jit(solution)/shard_map/all_to_all | solution.py:13
  125.6 3.1 %exponential_reduce_fusion.2 = f32[1024]{0:T(1024)S(1)} fusion(f32[1024,1024]{0,1:T(8,128)} %copy-done, f32[1024]{0:T(1024)S(1)} %bitcast_subtract_fusion.3, f32[1024]{0:T(1024)S(1)} %negate_bitcast_fusion), kind=kLoop, calls=%fused_computation.3 | loop fusion | flops 3144704 | bytes 4206592 | tf_op jit(solution)/shard_map/reduce_sum | solution.py:52
  128.7 10.5 %all_to_all.52 = f32[16,8,128]{2,1,0:T(8,128)S(1)} all-to-all(f32[16,8,128]{2,1,0:T(8,128)S(1)} %broadcast_in_dim.28), channel_id=1, replica_groups=mesh['src'=16,'tgt'=32] {'src'}, dimensions={0} | all-to-all | bytes 131072 | tf_op jit(solution)/shard_map/all_to_all | solution.py:13
  139.2 2.9 %exponential_reduce_fusion.1 = f32[1024]{0:T(1024)S(1)} fusion(f32[1024,1024]{0,1:T(8,128)} %copy-done, f32[1024]{0:T(1024)S(1)} %bitcast_subtract_fusion.2, f32[1024]{0:T(1024)S(1)} %bitcast_subtract_fusion.3), kind=kLoop, calls=%fused_computation.2 | loop fusion | flops 3144704 | bytes 4206592 | tf_op jit(solution)/shard_map/reduce_sum | solution.py:50
  142.2 14.2 %all_to_all.53 = f32[32,8,128]{2,1,0:T(8,128)S(1)} all-to-all(f32[32,8,128]{2,1,0:T(8,128)S(1)} %broadcast_in_dim.30), channel_id=1, replica_groups=mesh['src'=16,'tgt'=32] {'tgt'}, dimensions={0} | all-to-all | bytes 262144 | tf_op jit(solution)/shard_map/all_to_all | solution.py:13
  156.5 0.0 copy-start.2
  156.5 3.2 %exponential_reduce_fusion = f32[1024]{0:T(1024)S(1)} fusion(f32[1024,1024]{0,1:T(8,128)} %copy-done, f32[1024]{0:T(1024)S(1)} %bitcast_subtract_fusion.1, f32[1024]{0:T(1024)S(1)} %bitcast_subtract_fusion.2), kind=kLoop, calls=%fused_computation.1 | loop fusion | flops 3144704 | bytes 4206592 | tf_op jit(solution)/shard_map/reduce_sum | solution.py:52
  159.7 10.5 %all_to_all.54 = f32[16,8,128]{2,1,0:T(8,128)S(1)} all-to-all(f32[16,8,128]{2,1,0:T(8,128)S(1)} %broadcast_in_dim.32), channel_id=1, replica_groups=mesh['src'=16,'tgt'=32] {'src'}, dimensions={0} | all-to-all | bytes 131072 | tf_op jit(solution)/shard_map/all_to_all | solution.py:13
  170.2 0.6 broadcast_multiply_fusion
  170.8 2.9 %fusion = f32[1024]{0:T(1024)S(1)} fusion(f32[1024,1024]{0,1:T(8,128)} %copy-done, f32[1024]{0:T(1024)S(1)} %get-tuple-element.3, f32[1024]{0:T(1024)S(1)} %bitcast_subtract_fusion.1), kind=kLoop, calls=%fused_computation.9 | loop fusion | flops 3144704 | bytes 4206592 | tf_op jit(solution)/shard_map/reduce_sum | solution.py:55
  173.8 0.7 all_to_all.38
  174.5 4.0 %all-to-all-start.8 = ((f32[32,1,32]{2,1,0:T(1,128)}), f32[32,1,32]{2,1,0:T(1,128)S(1)}, u32[]{:S(2)}, u32[]{:S(2)}) async-start(f32[32,1,32]{2,1,0:T(1,128)} %all_to_all.38), calls=%async_computation.8 | async-start | bytes 32768 | tf_op jit(solution)/shard_map/all_to_all | solution.py:61
  178.5 0.0 copy-done.2
  178.5 16.3 %fusion.1 = f32[1024,384]{1,0:T(8,128)} fusion(f32[1024,384]{0,1:T(8,128)S(1)} %copy-done.2, f32[1024,1024]{0,1:T(8,128)} %copy-done, f32[1024]{0:T(1024)S(1)} %get-tuple-element.3, f32[1024]{0:T(1024)S(1)} %bitcast_subtract_fusion.1), kind=kOutput, calls=%fused_computation.10 | convolution fusion | flops 4833935360 | bytes 7348224 | tf_op jit(solution)/shard_map/dot_general | solution.py:56
  194.9 0.0 copy-start.3
  194.9 0.0 all-to-all-done.8
  194.9 9.7 %all-to-all-start.7 = ((f32[32,32,384]{2,1,0:T(8,128)}), f32[32,32,384]{2,1,0:T(8,128)S(1)}, u32[]{:S(2)}, u32[]{:S(2)}) async-start(f32[32,32,384]{2,1,0:T(8,128)} %bitcast.13), calls=%async_computation.7 | async-start | bytes 3145728 | tf_op jit(solution)/shard_map/all_to_all | solution.py:60
  204.6 39.4 %all-to-all-done.7 = f32[32,32,384]{2,1,0:T(8,128)S(1)} async-done(((f32[32,32,384]{2,1,0:T(8,128)}), f32[32,32,384]{2,1,0:T(8,128)S(1)}, u32[]{:S(2)}, u32[]{:S(2)}) %all-to-all-start.7) | async-done | bytes 1572896 | tf_op jit(solution)/shard_map/all_to_all | solution.py:60
  244.0 0.1 reduce_sum.167
  244.1 0.0 copy-done.3
  244.1 0.7 divide_subtract_fusion
  (22 shorter events, 0.4 us)
Async XLA Ops:
  7.2 48.4 %all-gather.2.cloned.1.call-start = ((), (), s32[]{:S(2)}) async-start(), calls=%async_computation.9 | async-start | bytes 1671168 | tf_op jit(solution)/shard_map/all_gather | solution.py:29
  10.0 52.5 %all-to-all-start = ((f32[32,32,384]{2,1,0:T(8,128)}), f32[32,32,384]{2,1,0:T(8,128)S(1)}, u32[]{:S(2)}, u32[]{:S(2)}) async-start(f32[32,32,384]{2,1,0:T(8,128)} %broadcast_in_dim.22), calls=%async_computation | async-start | bytes 3145728 | tf_op jit(solution)/shard_map/all_to_all | solution.py:13
  71.7 1.9 copy-start
  90.1 3.4 %copy-start.1 = (f32[1024,1024]{0,1:T(8,128)S(1)}, f32[1024,1024]{0,1:T(8,128)}, u32[]{:S(2)}) copy-start(f32[1024,1024]{0,1:T(8,128)} %copy-done) | copy-start | bytes 12582916
  156.5 22.0 %copy-start.2 = (f32[1024,384]{0,1:T(8,128)S(1)}, f32[1024,384]{0,1:T(8,128)}, u32[]{:S(2)}) copy-start(f32[1024,384]{0,1:T(8,128)} %all-gather.2.cloned.1.call-done) | copy-start | bytes 4718596
  174.5 20.4 %all-to-all-start.8 = ((f32[32,1,32]{2,1,0:T(1,128)}), f32[32,1,32]{2,1,0:T(1,128)S(1)}, u32[]{:S(2)}, u32[]{:S(2)}) async-start(f32[32,1,32]{2,1,0:T(1,128)} %all_to_all.38), calls=%async_computation.8 | async-start | bytes 32768 | tf_op jit(solution)/shard_map/all_to_all | solution.py:61
  194.9 49.3 %copy-start.3 = (f32[32,384]{1,0:T(8,128)S(1)}, f32[32,384]{1,0:T(8,128)}, u32[]{:S(2)}) copy-start(f32[32,384]{1,0:T(8,128)} %param.2) | copy-start | bytes 147460
  194.9 49.2 %all-to-all-start.7 = ((f32[32,32,384]{2,1,0:T(8,128)}), f32[32,32,384]{2,1,0:T(8,128)S(1)}, u32[]{:S(2)}, u32[]{:S(2)}) async-start(f32[32,32,384]{2,1,0:T(8,128)} %bitcast.13), calls=%async_computation.7 | async-start | bytes 3145728 | tf_op jit(solution)/shard_map/all_to_all | solution.py:60
Sparse Core Ops, SparseCore 0:
  10.1 45.4 all-gather.1
where the time goes:
time: 253 us; the launch traced here: 252 us
  blocking collectives  79.1 us (31%)
  waiting for transfers between devices  77.9 us (31%)
  starting transfers between devices  27 us (11%)
  matrix products  25.2 us (10%)
  other arithmetic  22.7 us (9%)
  between operations  14.2 us (6%)
  local copies, waits for them, and re-layouts  5.58 us (2%)
    all_to_all x6, blocking collectives, spread(): lax.all_to_all(jnp.broadcast_to(value[None], (count,) + value.shape), axi...  79.1 us
    all_to_all x1, waiting for transfers between devices, per_device(): lax.all_to_all(part.reshape(count, own_rows, feat_width), 'tgt', 0, 0)  39.4 us
    all_gather x1, waiting for transfers between devices, per_device(): target_rows = lax.all_gather(data, 'src', axis=1, tiled=True)  32.4 us
    dot_general x1, matrix products, per_device(): jnp.dot(plan, target_rows, precision=lax.Precision.HIGHEST, preferred_ele...  16.3 us
    all_to_all x1, starting transfers between devices, spread(): lax.all_to_all(jnp.broadcast_to(value[None], (count,) + value.shape), axi...  13.2 us
    all_to_all x1, starting transfers between devices, per_device(): lax.all_to_all(part.reshape(count, own_rows, feat_width), 'tgt', 0, 0)  9.7 us
    dot_general x1, matrix products, per_device(): jnp.dot(source_rows, target_rows.T, precision=lax.Precision.HIGHEST, pref...  8.88 us
    reduce_sum x2, other arithmetic, per_device(): mass = jnp.sum(jnp.exp(f_pot[:, None] + gain + g_pot[None, :]), axis=0)  6.26 us
  transfers between devices with their start and end apart: 4, of which 3 were waited for; matrix products, arithmetic and copies ran while one was open for 8% of the time, Pallas kernels for 0%

commit v1 on v0

--- a/solution.py
+++ b/solution.py
@@ -26,7 +26,9 @@
 
 
 def per_device(noise, data):
-    target_rows = lax.all_gather(data, "src", axis=1, tiled=True)
+    target_rows = jnp.concatenate(
+        lax.all_to_all(jnp.stack([data] * lax.axis_size("src")), "src", 0, 0), axis=1
+    )
     own_rows, feat_width = noise.shape
     source_rows = spread(noise, "tgt").reshape(-1, feat_width)
     src_total = source_rows.shape[0] * lax.axis_size("src")

time: 253 us -> 276 us (1.091)
  blocking collectives: 79.1 us -> 123 us
  between operations: 14.2 us -> 0.81 us
  matrix products: 25.2 us -> 17 us
    all_to_all x0 -> x1, blocking collectives: none -> 44.9 us  [per_device(): lax.all_to_all(jnp.stack([data] * lax.axis_size('src')), 'src', 0, 0)]
    all_to_all x1, waiting for transfers between devices: 5.41 us -> 39.7 us  [spread(): lax.all_to_all(jnp.broadcast_to(value[None], (count,) + value.shape), axi...]
    all_gather x1 -> x0, waiting for transfers between devices: 32.4 us -> none  [per_device(): target_rows = lax.all_gather(data, 'src', axis=1, tiled=True)]
    dot_general x1, matrix products: 16.3 us -> 9.53 us  [per_device(): jnp.dot(plan, target_rows, precision=lax.Precision.HIGHEST, preferred_ele...]
  transfers between devices with their start and end apart: 4 -> 3, of which waited for: 3 -> 3; matrix products, arithmetic and copies ran while one was open for 8% -> 4% of each run, Pallas kernels for 0% -> 0%
where the time goes in v1:
time: 276 us; the launch traced here: 275 us
  blocking collectives  123 us (45%)
  waiting for transfers between devices  79.3 us (29%)
  starting transfers between devices  25.7 us (9%)
  other arithmetic  23.6 us (9%)
  matrix products  17 us (6%)
  local copies, waits for them, and re-layouts  5.9 us (2%)
    all_to_all x6, blocking collectives, spread(): lax.all_to_all(jnp.broadcast_to(value[None], (count,) + value.shape), axi...  77.6 us
    all_to_all x1, blocking collectives, per_device(): lax.all_to_all(jnp.stack([data] * lax.axis_size('src')), 'src', 0, 0)  44.9 us
    all_to_all x1, waiting for transfers between devices, spread(): lax.all_to_all(jnp.broadcast_to(value[None], (count,) + value.shape), axi...  39.7 us
    all_to_all x1, waiting for transfers between devices, per_device(): lax.all_to_all(part.reshape(count, own_rows, feat_width), 'tgt', 0, 0)  39.4 us
    all_to_all x1, starting transfers between devices, spread(): lax.all_to_all(jnp.broadcast_to(value[None], (count,) + value.shape), axi...  12.3 us
    all_to_all x1, starting transfers between devices, per_device(): lax.all_to_all(part.reshape(count, own_rows, feat_width), 'tgt', 0, 0)  9.58 us
    dot_general x1, matrix products, per_device(): jnp.dot(plan, target_rows, precision=lax.Precision.HIGHEST, preferred_ele...  9.53 us
    dot_general x1, matrix products, per_device(): jnp.dot(source_rows, target_rows.T, precision=lax.Precision.HIGHEST, pref...  7.47 us
  transfers between devices with their start and end apart: 3, of which 3 were waited for; matrix products, arithmetic and copies ran while one was open for 4% of the time, Pallas kernels for 0%

profile of v1, /device:TPU:8, one launch (start us, length us, event | category | flops | bytes accessed | tf_op | source)
XLA Modules:
  0.0 274.8 jit_solution(12714504499150397524)
XLA Ops:
  0.6 0.0 copy-start.2
  0.6 1.1 stack.2
  1.7 44.9 %all_to_all.54 = f32[16,1024,24]{1,2,0:T(8,128)S(1)} all-to-all(f32[16,1024,24]{1,2,0:T(8,128)S(1)} %stack.2), channel_id=1, replica_groups=mesh['src'=16,'tgt'=32] {'src'}, dimensions={0} | all-to-all | bytes 3145728 | tf_op jit(solution)/shard_map/all_to_all | solution.py:30
  46.7 0.0 copy-done.2
  46.7 1.3 broadcast_in_dim.22
  48.0 12.3 %all-to-all-start = ((f32[32,32,384]{2,1,0:T(8,128)}), f32[32,32,384]{2,1,0:T(8,128)S(1)}, u32[]{:S(2)}, u32[]{:S(2)}) async-start(f32[32,32,384]{2,1,0:T(8,128)} %broadcast_in_dim.22), calls=%async_computation | async-start | bytes 3145728 | tf_op jit(solution)/shard_map/all_to_all | solution.py:13
  60.3 0.1 fusion
  60.4 39.7 %all-to-all-done = f32[32,32,384]{2,1,0:T(8,128)S(1)} async-done(((f32[32,32,384]{2,1,0:T(8,128)}), f32[32,32,384]{2,1,0:T(8,128)S(1)}, u32[]{:S(2)}, u32[]{:S(2)}) %all-to-all-start) | async-done | bytes 1572896 | tf_op jit(solution)/shard_map/all_to_all | solution.py:13
  100.1 0.2 multiply_reduce_fusion
  100.3 0.1 sub.87
  100.4 7.5 %fusion.2 = (f32[1024]{0:T(1024)S(1)}, f32[1024,1024]{1,0:T(8,128)S(1)}) fusion(f32[1024]{0:T(1024)S(1)} %fusion, f32[1024]{0:T(1024)S(1)} %sub.87, f32[1024,384]{1,0:T(8,128)S(1)} %bitcast.39, f32[1024,384]{0,1:T(8,128)S(1)} %bitcast.37), kind=kOutput, calls=%fused_computation.25 | convolution fusion | flops 4837080064 | bytes 7352320 | tf_op jit(solution)/shard_map/dot_general | solution.py:38
  107.9 0.0 copy-start
  107.9 2.0 copy-done
  109.8 1.1 exponential_reduce_fusion.5
  110.9 15.9 %all_to_all.55 = f32[32,8,128]{2,1,0:T(8,128)S(1)} all-to-all(f32[32,8,128]{2,1,0:T(8,128)S(1)} %broadcast_in_dim.23), channel_id=1, replica_groups=mesh['src'=16,'tgt'=32] {'tgt'}, dimensions={0} | all-to-all | bytes 262144 | tf_op jit(solution)/shard_map/all_to_all | solution.py:13
  126.8 0.0 copy-start.1
  126.9 2.7 add_reduce_fusion
  129.6 0.7 copy-done.1
  130.3 0.8 exponential_reduce_fusion.4
  131.1 12.2 %all_to_all.56 = f32[16,8,128]{2,1,0:T(8,128)S(1)} all-to-all(f32[16,8,128]{2,1,0:T(8,128)S(1)} %broadcast_in_dim.24), channel_id=1, replica_groups=mesh['src'=16,'tgt'=32] {'src'}, dimensions={0} | all-to-all | bytes 131072 | tf_op jit(solution)/shard_map/all_to_all | solution.py:13
  143.4 3.1 %exponential_reduce_fusion.3 = f32[1024]{0:T(1024)S(1)} fusion(f32[1024,1024]{1,0:T(8,128)} %copy-done, f32[1024]{0:T(1024)S(1)} %negate_bitcast_fusion, f32[1024]{0:T(1024)S(1)} %negate_bitcast_fusion.1), kind=kLoop, calls=%fused_computation.4 | loop fusion | flops 3144704 | bytes 4206592 | tf_op jit(solution)/shard_map/reduce_sum | solution.py:52
  146.5 14.2 %all_to_all.57 = f32[32,8,128]{2,1,0:T(8,128)S(1)} all-to-all(f32[32,8,128]{2,1,0:T(8,128)S(1)} %broadcast_in_dim.26), channel_id=1, replica_groups=mesh['src'=16,'tgt'=32] {'tgt'}, dimensions={0} | all-to-all | bytes 262144 | tf_op jit(solution)/shard_map/all_to_all | solution.py:13
  160.8 3.0 %exponential_reduce_fusion.2 = f32[1024]{0:T(1024)S(1)} fusion(f32[1024,1024]{1,0:T(8,128)} %copy-done, f32[1024]{0:T(1024)S(1)} %bitcast_subtract_fusion.3, f32[1024]{0:T(1024)S(1)} %negate_bitcast_fusion), kind=kLoop, calls=%fused_computation.3 | loop fusion | flops 3144704 | bytes 4206592 | tf_op jit(solution)/shard_map/reduce_sum | solution.py:54
  163.8 10.5 %all_to_all.58 = f32[16,8,128]{2,1,0:T(8,128)S(1)} all-to-all(f32[16,8,128]{2,1,0:T(8,128)S(1)} %broadcast_in_dim.28), channel_id=1, replica_groups=mesh['src'=16,'tgt'=32] {'src'}, dimensions={0} | all-to-all | bytes 131072 | tf_op jit(solution)/shard_map/all_to_all | solution.py:13
  174.3 3.1 %exponential_reduce_fusion.1 = f32[1024]{0:T(1024)S(1)} fusion(f32[1024,1024]{1,0:T(8,128)} %copy-done, f32[1024]{0:T(1024)S(1)} %bitcast_subtract_fusion.2, f32[1024]{0:T(1024)S(1)} %bitcast_subtract_fusion.3), kind=kLoop, calls=%fused_computation.2 | loop fusion | flops 3144704 | bytes 4206592 | tf_op jit(solution)/shard_map/reduce_sum | solution.py:52
  177.4 14.2 %all_to_all.59 = f32[32,8,128]{2,1,0:T(8,128)S(1)} all-to-all(f32[32,8,128]{2,1,0:T(8,128)S(1)} %broadcast_in_dim.30), channel_id=1, replica_groups=mesh['src'=16,'tgt'=32] {'tgt'}, dimensions={0} | all-to-all | bytes 262144 | tf_op jit(solution)/shard_map/all_to_all | solution.py:13
  191.7 2.9 %exponential_reduce_fusion = f32[1024]{0:T(1024)S(1)} fusion(f32[1024,1024]{1,0:T(8,128)} %copy-done, f32[1024]{0:T(1024)S(1)} %bitcast_subtract_fusion.1, f32[1024]{0:T(1024)S(1)} %bitcast_subtract_fusion.2), kind=kLoop, calls=%fused_computation.1 | loop fusion | flops 3144704 | bytes 4206592 | tf_op jit(solution)/shard_map/reduce_sum | solution.py:54
  194.7 10.5 %all_to_all.60 = f32[16,8,128]{2,1,0:T(8,128)S(1)} all-to-all(f32[16,8,128]{2,1,0:T(8,128)S(1)} %broadcast_in_dim.32), channel_id=1, replica_groups=mesh['src'=16,'tgt'=32] {'src'}, dimensions={0} | all-to-all | bytes 131072 | tf_op jit(solution)/shard_map/all_to_all | solution.py:13
  205.2 0.6 broadcast_multiply_fusion
  205.8 4.9 %fusion.1 = (f32[1024]{0:T(1024)S(1)}, f32[1024,1024]{1,0:T(8,128)}) fusion(f32[1024]{0:T(1024)S(1)} %get-tuple-element.3, f32[1024,1024]{1,0:T(8,128)} %copy-done, f32[1024]{0:T(1024)S(1)} %bitcast_subtract_fusion.1), kind=kLoop, calls=%fused_computation.24 | loop fusion | flops 3144704 | bytes 8400896 | tf_op jit(solution)/shard_map/reduce_sum | solution.py:57
  210.7 0.7 all_to_all.42
  211.4 3.8 %all-to-all-start.9 = ((f32[32,1,32]{2,1,0:T(1,128)}), f32[32,1,32]{2,1,0:T(1,128)S(1)}, u32[]{:S(2)}, u32[]{:S(2)}) async-start(f32[32,1,32]{2,1,0:T(1,128)} %all_to_all.42), calls=%async_computation.9 | async-start | bytes 32768 | tf_op jit(solution)/shard_map/all_to_all | solution.py:63
  215.3 9.5 %fusion.3 = f32[32,32,384]{2,1,0:T(8,128)} fusion(f32[32,32,1024]{2,1,0:T(8,128)} %bitcast.36, f32[1024,384,1]{0,1,2:T(8,128)S(1)} %bitcast.38), kind=kOutput, calls=%fused_computation.26 | convolution fusion | flops 4831838208 | bytes 7340032 | tf_op jit(solution)/shard_map/dot_general | solution.py:58
  224.8 0.2 all-to-all-done.9
  225.0 9.6 %all-to-all-start.8 = ((f32[32,32,384]{2,1,0:T(8,128)}), f32[32,32,384]{2,1,0:T(8,128)S(1)}, u32[]{:S(2)}, u32[]{:S(2)}) async-start(f32[32,32,384]{2,1,0:T(8,128)} %fusion.3), calls=%async_computation.8 | async-start | bytes 3145728 | tf_op jit(solution)/shard_map/all_to_all | solution.py:62
  234.6 39.4 %all-to-all-done.8 = f32[32,32,384]{2,1,0:T(8,128)S(1)} async-done(((f32[32,32,384]{2,1,0:T(8,128)}), f32[32,32,384]{2,1,0:T(8,128)S(1)}, u32[]{:S(2)}, u32[]{:S(2)}) %all-to-all-start.8) | async-done | bytes 1572896 | tf_op jit(solution)/shard_map/all_to_all | solution.py:62
  274.0 0.1 reduce_sum.167
  274.1 0.7 divide_subtract_fusion
  (22 shorter events, 0.4 us)
Async XLA Ops:
  0.6 46.0 %copy-start.2 = (f32[32,384]{1,0:T(8,128)S(1)}, f32[32,384]{1,0:T(8,128)}, u32[]{:S(2)}) copy-start(f32[32,384]{1,0:T(8,128)} %param.2) | copy-start | bytes 147460
  48.0 52.1 %all-to-all-start = ((f32[32,32,384]{2,1,0:T(8,128)}), f32[32,32,384]{2,1,0:T(8,128)S(1)}, u32[]{:S(2)}, u32[]{:S(2)}) async-start(f32[32,32,384]{2,1,0:T(8,128)} %broadcast_in_dim.22), calls=%async_computation | async-start | bytes 3145728 | tf_op jit(solution)/shard_map/all_to_all | solution.py:13
  107.9 2.0 copy-start
  126.8 3.4 %copy-start.1 = (f32[1024,1024]{1,0:T(8,128)S(1)}, f32[1024,1024]{1,0:T(8,128)}, u32[]{:S(2)}) copy-start(f32[1024,1024]{1,0:T(8,128)} %copy-done) | copy-start | bytes 12582916
  211.4 13.6 %all-to-all-start.9 = ((f32[32,1,32]{2,1,0:T(1,128)}), f32[32,1,32]{2,1,0:T(1,128)S(1)}, u32[]{:S(2)}, u32[]{:S(2)}) async-start(f32[32,1,32]{2,1,0:T(1,128)} %all_to_all.42), calls=%async_computation.9 | async-start | bytes 32768 | tf_op jit(solution)/shard_map/all_to_all | solution.py:63
  225.0 49.0 %all-to-all-start.8 = ((f32[32,32,384]{2,1,0:T(8,128)}), f32[32,32,384]{2,1,0:T(8,128)S(1)}, u32[]{:S(2)}, u32[]{:S(2)}) async-start(f32[32,32,384]{2,1,0:T(8,128)} %fusion.3), calls=%async_computation.8 | async-start | bytes 3145728 | tf_op jit(solution)/shard_map/all_to_all | solution.py:62
